TPU v7x, 256 devices: a whole 4x4x8 slice. The times are simulated.
256 devices in a mesh: grp: 8 (over z), slab: 32 (over y, x, core).
Axes of the slice: x: 4, y: 4, z: 8, core: 2. Of those that a mesh axis runs over, the one named last changes fastest.
Arguments:
- spectra: bfloat16 [131072, 2048], P(('grp', 'slab')), may hold values from -6 to 6
- ctf_sq: bfloat16 [131072, 1024], P(('grp', 'slab')), may hold values from 0.049804688 to 1
- dest: int32 [131072, 1], P(('grp', 'slab')), may hold values from 0 to 31; in each aligned block of 512 rows (0 to 511, 512 to 1023, ...) at most 32 rows name the same one
- block: int32 [131072], P(('grp', 'slab')), may hold values from 0 to 63
- pattern: int32 [131072], P(('grp', 'slab')), may hold values from 0 to 63
- pattern_table: bfloat16 [64, 8], replicated, may hold values from 0.049804688 to 1
- tau: float32 [1024], replicated, may hold values from 0.5 to 4
Outputs:
- image: float32 [2, 16, 1024, 1024], P(None, 'grp', None, 'slab')
Inputs may be any that keep to these rules, and one draw needn't show every extreme that they name: `dest`: among the rows of one device at most 32 name the same slab; in some device's rows one slab is named by exactly 32.
All inputs are finite; a program needn't handle non-finite values.
Results may differ from a plain program's by a relative error of at most 0.0003.
Values may be sent and summed in bfloat16 or wider, within the bound.
A program may use at most 192 MiB of HBM per device.

v0:
```python
import math
import jax
import jax.numpy as jnp
from jax import lax
from jax.sharding import PartitionSpec as P

KZ_DEV = 32
YWIN = 16
NBLK = 64


def dft_tables(length):
    indices = jnp.arange(length, dtype=jnp.int32)
    product = indices[:, None] * indices[None, :] % length
    angles = product.astype(jnp.float32) * (2.0 * math.pi / length)
    return (jnp.cos(angles), jnp.sin(angles))


def inverse_kz(filtered, cosine, sine):
    real_part = filtered[:, :, 0, :]
    imag_part = filtered[:, :, 1, :]
    scaling = 1.0 / math.sqrt(cosine.shape[0])
    highest = lax.Precision.HIGHEST
    out_real = jnp.einsum("zk,ykx->yzx", cosine, real_part, precision=highest) - jnp.einsum(
        "zk,ykx->yzx", sine, imag_part, precision=highest
    )
    out_imag = jnp.einsum("zk,ykx->yzx", sine, real_part, precision=highest) + jnp.einsum(
        "zk,ykx->yzx", cosine, imag_part, precision=highest
    )
    return jnp.stack([out_real * scaling, out_imag * scaling])


def on_device(spectra, ctf_sq, dest, block, pattern, pattern_table, tau):
    slab_count = lax.axis_size("slab")
    rows_here = spectra.shape[0]
    kx_width = ctf_sq.shape[1]
    spread = pattern_table.shape[1]
    capacity = max(2, 2 * rows_here // slab_count)
    slot_total = slab_count * capacity
    slab_ids = jnp.arange(slab_count, dtype=jnp.int32)
    matches = (dest == slab_ids[None, :]).astype(jnp.int32)
    earlier = jnp.cumsum(matches, axis=0) - matches
    position = jnp.sum(earlier * matches, axis=1)
    target = dest[:, 0] * capacity + position
    pattern_ids = jnp.arange(pattern_table.shape[0], dtype=jnp.int32)
    pattern_onehot = (pattern[:, None] == pattern_ids[None, :]).astype(jnp.bfloat16)
    row_weights = jnp.dot(pattern_onehot, pattern_table, preferred_element_type=jnp.float32).astype(
        jnp.bfloat16
    )
    block_label = (block + 1).astype(jnp.float32).astype(jnp.bfloat16)[:, None]
    send_spec = jnp.zeros((slot_total, 2 * kx_width), jnp.bfloat16).at[target].set(spectra)
    send_ctf = jnp.zeros((slot_total, kx_width), jnp.bfloat16).at[target].set(ctf_sq)
    send_weights = jnp.zeros((slot_total, spread), jnp.bfloat16).at[target].set(row_weights)
    send_label = jnp.zeros((slot_total, 1), jnp.bfloat16).at[target].set(block_label)
    got_spec, got_ctf, got_weights, got_label = (
        lax.all_to_all(send_spec, "slab", split_axis=0, concat_axis=0, tiled=True),
        lax.all_to_all(send_ctf, "slab", split_axis=0, concat_axis=0, tiled=True),
        lax.all_to_all(send_weights, "slab", split_axis=0, concat_axis=0, tiled=True),
        lax.all_to_all(send_label, "slab", split_axis=0, concat_axis=0, tiled=True),
    )
    block_ids = jnp.arange(1, NBLK + 1, dtype=jnp.int32).astype(jnp.float32)
    block_match = (got_label.astype(jnp.float32) == block_ids[None, :]).astype(jnp.bfloat16)
    spreader = (block_match[:, :, None] * got_weights[:, None, :]).reshape(
        slot_total, NBLK * spread
    )
    contract = (((0,), (0,)), ((), ()))
    cosine, sine = dft_tables(KZ_DEV * slab_count)
    column_width = kx_width // slab_count
    data_sum = lax.dot_general(spreader, got_spec, contract, preferred_element_type=jnp.float32)
    weight_sum = lax.dot_general(spreader, got_ctf, contract, preferred_element_type=jnp.float32)
    data_sum = data_sum.reshape(YWIN, KZ_DEV, 2, kx_width)
    weight_sum = weight_sum.reshape(YWIN, KZ_DEV, 1, kx_width)
    volume = jnp.concatenate([data_sum, weight_sum], axis=2)
    columns_all = lax.all_to_all(volume, "slab", split_axis=3, concat_axis=1, tiled=True)
    summed = lax.psum_scatter(columns_all, "grp", scatter_dimension=0, tiled=True)
    tau_part = lax.dynamic_slice_in_dim(tau, lax.axis_index("slab") * column_width, column_width, 0)
    filtered = summed[:, :, 0:2, :] / (summed[:, :, 2:3, :] + tau_part[None, None, None, :])
    image = inverse_kz(filtered, cosine, sine)
    return image


def solution(mesh):
    in_specs = (
        P(("grp", "slab"), None),
        P(("grp", "slab"), None),
        P(("grp", "slab"), None),
        P(("grp", "slab")),
        P(("grp", "slab")),
        P(),
        P(),
    )
    out_specs = P(None, "grp", None, "slab")
    return jax.shard_map(
        on_device, mesh=mesh, in_specs=in_specs, out_specs=out_specs, check_vma=False
    )
```

profile of v0, /device:TPU:1, one launch (start us, length us, event | category | flops | bytes accessed | tf_op | source)
XLA Modules:
  0.0 599.7 jit_solution(15534419843716490866)
XLA Ops:
  6.5 0.0 copy-start
  6.5 0.7 fusion.49
  7.2 1.2 reduce-window.6
  8.4 0.2 slice_reduce_fusion
  8.7 0.8 fusion.48
  9.4 0.7 compare_select_fusion
  10.1 0.7 convert_convert_fusion
  10.8 3.8 scatter_custom_fusion
  14.6 0.7 all_to_all.55
  15.3 8.6 %all-to-all-start = ((bf16[32,32,1]{1,2,0:T(2,128)(2,1)}), bf16[32,32,1]{1,2,0:T(2,128)(2,1)S(1)}, u32[]{:S(2)}, u32[]{:S(2)}) async-start(bf16[32,32,1]{1,2,0:T(2,128)(2,1)} %all_to_all.55), calls=%async_computation | async-start | bytes 32768 | tf_op jit(solution)/shard_map/all_to_all | solution.py:59
  23.9 0.0 copy-done
  23.9 0.9 convolution_convert_fusion
  24.8 0.2 copy.31
  25.0 1.8 scatter_custom_fusion.1
  26.8 0.1 copy.32
  27.0 0.7 reshape.148
  27.7 3.1 all-to-all-done
  30.8 4.2 all-to-all-start.1
  35.1 4.8 scatter_custom_fusion.3
  39.9 2.1 all-to-all-done.1
  42.0 5.7 all-to-all-start.3
  47.7 7.3 %scatter_custom_fusion.2 = bf16[1024,2048]{1,0:T(8,128)(2,1)} fusion(s32[512]{0:T(512)S(1)} %bitcast.129, bf16[512,2048]{1,0:T(8,128)(2,1)} %param.7, bf16[]{:T(256)} %constant.12.clone.1), kind=kCustom, calls=%fused_computation.24 | custom fusion | bytes 4194816 | tf_op jit(solution)/shard_map/scatter | solution.py:51
  55.0 21.3 %all-to-all-done.3 = bf16[32,32,1024]{2,1,0:T(8,128)(2,1)S(1)} async-done(((bf16[32,32,1024]{2,1,0:T(8,128)(2,1)}), bf16[32,32,1024]{2,1,0:T(8,128)(2,1)S(1)}, u32[]{:S(2)}, u32[]{:S(2)}) %all-to-all-start.3) | async-done | bytes 2097184 | tf_op jit(solution)/shard_map/all_to_all | solution.py:57
  76.2 6.1 %all-to-all-start.2 = ((bf16[32,32,2048]{2,1,0:T(8,128)(2,1)}), bf16[32,32,2048]{2,1,0:T(8,128)(2,1)}, u32[]{:S(2)}, u32[]{:S(2)}) async-start(bf16[32,32,2048]{2,1,0:T(8,128)(2,1)} %bitcast.115), calls=%async_computation.2 | async-start | bytes 8388608 | tf_op jit(solution)/shard_map/all_to_all | solution.py:56
  82.3 0.0 all-reduce.3.cloned.1.call-start
  82.4 0.1 convert_reduce_fusion
  82.4 0.1 reshape.87
  82.5 0.1 compare_convert_fusion
  82.6 0.1 reshape.149
  82.7 0.1 mul.91
  82.9 0.1 broadcast_multiply_fusion
  83.0 2.7 convolution_bitcast_fusion
  85.7 47.4 %all-to-all-done.2 = bf16[32,32,2048]{2,1,0:T(8,128)(2,1)} async-done(((bf16[32,32,2048]{2,1,0:T(8,128)(2,1)}), bf16[32,32,2048]{2,1,0:T(8,128)(2,1)}, u32[]{:S(2)}, u32[]{:S(2)}) %all-to-all-start.2) | async-done | bytes 4194336 | tf_op jit(solution)/shard_map/all_to_all | solution.py:56
  133.0 6.4 %copy.34 = bf16[2048,1024]{1,0:T(8,128)(2,1)} copy(bf16[2048,1024]{0,1:T(8,128)(2,1)} %bitcast.13) | data formatting | bytes 8388608 | tf_op jit(solution)/shard_map/dot_general | solution.py:69
  139.4 0.0 copy-start.2
  139.4 4.7 fusion.68
  144.1 0.0 copy-done.2
  144.1 3.3 pad_maximum_fusion
  147.4 18.1 %copy.35 = f32[16,32,3,1024]{1,0,2,3:T(8,128)} copy(f32[16,32,3,1024]{3,1,2,0:T(8,128)} %pad_maximum_fusion) | data formatting | bytes 12582912 | tf_op jit(solution)/shard_map/concatenate | solution.py:73
  165.5 27.1 %reshape.150 = f32[32,1,49152]{2,1,0:T(1,128)} reshape(f32[1024,3,16,32]{3,2,1,0:T(8,128)} %bitcast.114) | data formatting | bytes 12582912
  192.7 82.1 %all_to_all.61 = f32[32,1,49152]{2,1,0:T(1,128)} all-to-all(f32[32,1,49152]{2,1,0:T(1,128)} %reshape.150), channel_id=1, replica_groups=mesh['grp'=8,'slab'=32] {'slab'}, dimensions={0} | all-to-all | bytes 12582912 | tf_op jit(solution)/shard_map/all_to_all | solution.py:74
  274.8 0.5 broadcast.112
  275.3 19.9 %reduce.6 = f32[32,49152]{1,0:T(8,128)} reduce(f32[32,1,49152]{2,1,0:T(1,128)} %all_to_all.61, f32[]{:T(128)} %broadcast.112), dimensions={1}, to_apply=%all_to_all.51.reduce_sub_computation | reduce | bytes 12582916 | tf_op jit(solution)/shard_map/all_to_all | solution.py:74
  295.2 24.4 %reshape.151 = f32[1024,3,16,32]{3,2,1,0:T(8,128)} reshape(f32[32,49152]{1,0:T(8,128)} %reduce.6) | data formatting | bytes 12582912
  319.6 24.7 %copy.36 = f32[16,32,32,3,32]{2,1,4,0,3:T(8,128)} copy(f32[16,32,32,3,32]{2,0,3,4,1:T(8,128)} %bitcast.113) | data formatting | bytes 12582912 | tf_op jit(solution)/shard_map/all_to_all | solution.py:74
  344.3 20.1 %all_to_all.54 = f32[16,1024,3,32]{1,3,0,2:T(8,128)} reshape(f32[16,32,32,3,32]{2,1,4,0,3:T(8,128)} %copy.36) | data formatting | bytes 12582912 | tf_op jit(solution)/shard_map/all_to_all | solution.py:74
  364.4 0.0 copy-start.3
  364.4 0.0 all-reduce.3.cloned.1.call-update
  364.4 0.8 dynamic_slice.3
  365.2 0.0 copy-done.3
  365.2 0.6 dynamic-slice
  366.4 146.4 %all-reduce.3.cloned.1.call-done = f32[16,1024,3,32]{1,3,0,2:T(8,128)} async-done(((f32[16,1024,3,32]{1,3,0,2:T(8,128)}), f32[16,1024,3,32]{1,3,0,2:T(8,128)}) %all-reduce.3.cloned.1.call-update) | async-done | bytes 6291472
  512.8 1.0 fusion.42
  513.9 1.1 dynamic-slice_divide_fusion
  515.0 19.1 %fusion.5 = f32[2,32,1024]{2,1,0:T(8,128)S(1)} fusion(f32[2,1024,2,32]{1,3,0,2:T(8,128)S(1)} %dynamic-slice_divide_fusion), kind=kOutput, calls=%fused_computation.13 | convolution fusion | flops 819986432 | bytes 524288 | tf_op jit(solution)/shard_map/zk,ykx->yzx/dot_general | solution.py:24
  534.1 19.4 %fusion.3 = f32[2,32,1024]{2,1,0:T(8,128)S(1)} fusion(f32[2,1024,2,32]{1,3,0,2:T(8,128)S(1)} %dynamic-slice_divide_fusion), kind=kOutput, calls=%fused_computation.11 | convolution fusion | flops 819986432 | bytes 524288 | tf_op jit(solution)/shard_map/zk,ykx->yzx/dot_general | solution.py:27
  553.5 19.0 %fusion.37 = f32[1,2,1024,32]{2,3,1,0:T(8,128)S(1)} fusion(f32[2,32,1024]{2,1,0:T(8,128)S(1)} %fusion.5, f32[2,1024,2,32]{1,3,0,2:T(8,128)S(1)} %dynamic-slice_divide_fusion), kind=kOutput, calls=%fused_computation.32 | convolution fusion | flops 820117504 | bytes 786432 | tf_op jit(solution)/shard_map/zk,ykx->yzx/dot_general | solution.py:24
  572.5 0.0 copy-start.1
  572.5 19.3 %fusion.31 = f32[1,2,1024,32]{2,3,1,0:T(8,128)S(1)} fusion(f32[2,32,1024]{2,1,0:T(8,128)S(1)} %fusion.3, f32[2,1024,2,32]{1,3,0,2:T(8,128)S(1)} %dynamic-slice_divide_fusion), kind=kOutput, calls=%fused_computation.30 | convolution fusion | flops 820117504 | bytes 786432 | tf_op jit(solution)/shard_map/zk,ykx->yzx/dot_general | solution.py:27
  591.8 0.8 pad_maximum_fusion.1
  592.6 0.0 copy-done.1
  (4 shorter events, 0.1 us)
Async XLA Ops:
  6.5 17.3 %copy-start = (bf16[64,8]{0,1:T(8,128)(2,1)S(1)}, bf16[64,8]{0,1:T(8,128)(2,1)}, u32[]{:S(2)}) copy-start(bf16[64,8]{0,1:T(8,128)(2,1)} %param.12) | copy-start | bytes 3076
  15.3 15.6 %all-to-all-start = ((bf16[32,32,1]{1,2,0:T(2,128)(2,1)}), bf16[32,32,1]{1,2,0:T(2,128)(2,1)S(1)}, u32[]{:S(2)}, u32[]{:S(2)}) async-start(bf16[32,32,1]{1,2,0:T(2,128)(2,1)} %all_to_all.55), calls=%async_computation | async-start | bytes 32768 | tf_op jit(solution)/shard_map/all_to_all | solution.py:59
  30.8 11.1 %all-to-all-start.1 = ((bf16[32,2,128]{2,1,0:T(2,128)(2,1)}), bf16[32,2,128]{2,1,0:T(2,128)(2,1)S(1)}, u32[]{:S(2)}, u32[]{:S(2)}) async-start(bf16[32,2,128]{2,1,0:T(2,128)(2,1)} %reshape.148), calls=%async_computation.1 | async-start | bytes 32768 | tf_op jit(solution)/shard_map/all_to_all | solution.py:58
  42.0 34.3 %all-to-all-start.3 = ((bf16[32,32,1024]{2,1,0:T(8,128)(2,1)}), bf16[32,32,1024]{2,1,0:T(8,128)(2,1)S(1)}, u32[]{:S(2)}, u32[]{:S(2)}) async-start(bf16[32,32,1024]{2,1,0:T(8,128)(2,1)} %bitcast.18), calls=%async_computation.3 | async-start | bytes 4194304 | tf_op jit(solution)/shard_map/all_to_all | solution.py:57
  76.2 56.8 %all-to-all-start.2 = ((bf16[32,32,2048]{2,1,0:T(8,128)(2,1)}), bf16[32,32,2048]{2,1,0:T(8,128)(2,1)}, u32[]{:S(2)}, u32[]{:S(2)}) async-start(bf16[32,32,2048]{2,1,0:T(8,128)(2,1)} %bitcast.115), calls=%async_computation.2 | async-start | bytes 8388608 | tf_op jit(solution)/shard_map/all_to_all | solution.py:56
  82.3 430.5 %all-reduce.3.cloned.1.call-start = ((), (), s32[]{:S(2)}) async-start(), calls=%async_computation.5 | async-start | bytes 12582912
  139.4 4.7 copy-start.2
  364.4 0.8 copy-start.3
  572.5 20.2 %copy-start.1 = (bf16[64,8]{0,1:T(8,128)(2,1)S(1)}, bf16[64,8]{0,1:T(8,128)(2,1)}, u32[]{:S(2)}) copy-start(bf16[64,8]{0,1:T(8,128)(2,1)} %param.12) | copy-start | bytes 3076
Sparse Core Ops, SparseCore 0:
  364.5 148.2 all-reduce.2
where the time goes:
time: 609 us; the launch traced here: 600 us
  waiting for transfers between devices  220 us (36%)
  local copies, waits for them, and re-layouts  143 us (23%)
  matrix products  85.1 us (14%)
  blocking collectives  82.1 us (13%)
  other arithmetic  30.5 us (5%)
  starting transfers between devices  24.7 us (4%)
  between operations  14.4 us (2%)
    unnamed x2, waiting for transfers between devices  146 us
    all_to_all x1, blocking collectives, on_device(): lax.all_to_all(volume, 'slab', split_axis=3, concat_axis=1, tiled=True)  82.1 us
    unnamed x13, local copies, waits for them, and re-layouts  52.9 us
    all_to_all x1, waiting for transfers between devices, on_device(): lax.all_to_all(send_spec, 'slab', split_axis=0, concat_axis=0, tiled=True)  47.4 us
    all_to_all x3, local copies, waits for them, and re-layouts, on_device(): lax.all_to_all(volume, 'slab', split_axis=3, concat_axis=1, tiled=True)  45.3 us
    all_to_all x1, waiting for transfers between devices, on_device(): lax.all_to_all(send_ctf, 'slab', split_axis=0, concat_axis=0, tiled=True)  21.3 us
    all_to_all x1, other arithmetic, on_device(): lax.all_to_all(volume, 'slab', split_axis=3, concat_axis=1, tiled=True)  19.9 us
    dot_general x1, matrix products, inverse_kz(): jnp.einsum('zk,ykx->yzx', sine, real_part, precision=highest)  19.4 us
  transfers between devices with their start and end apart: 5, of which 5 were waited for; matrix products, arithmetic and copies ran while one was open for 3% of the time, Pallas kernels for 0%

commit v1 on v0

--- a/solution.py
+++ b/solution.py
@@ -71,7 +71,10 @@
     data_sum = data_sum.reshape(YWIN, KZ_DEV, 2, kx_width)
     weight_sum = weight_sum.reshape(YWIN, KZ_DEV, 1, kx_width)
     volume = jnp.concatenate([data_sum, weight_sum], axis=2)
-    columns_all = lax.all_to_all(volume, "slab", split_axis=3, concat_axis=1, tiled=True)
+    columns_all = jnp.concatenate(
+        lax.all_to_all(jnp.stack(jnp.split(volume, lax.axis_size("slab"), axis=3)), "slab", 0, 0),
+        axis=1,
+    )
     summed = lax.psum_scatter(columns_all, "grp", scatter_dimension=0, tiled=True)
     tau_part = lax.dynamic_slice_in_dim(tau, lax.axis_index("slab") * column_width, column_width, 0)
     filtered = summed[:, :, 0:2, :] / (summed[:, :, 2:3, :] + tau_part[None, None, None, :])

time: 609 us -> 624 us (1.025)
  local copies, waits for them, and re-layouts: 143 us -> 153 us
    reshape x0 -> x3, local copies, waits for them, and re-layouts: none -> 65.2 us  [on_device(): jnp.concatenate(lax.all_to_all(jnp.stack(jnp.split(volume, lax.axis_size(...]
    all_to_all x3 -> x1, local copies, waits for them, and re-layouts: 45.3 us -> 0.51 us  [on_device(): lax.all_to_all(jnp.stack(jnp.split(volume, lax.axis_size('slab'), axis=3)...]
    concatenate x1 -> x0, local copies, waits for them, and re-layouts: 18.1 us -> none  [on_device(): volume = jnp.concatenate([data_sum, weight_sum], axis=2)]
    unnamed x13 -> x15, local copies, waits for them, and re-layouts: 52.9 us -> 61.4 us
    unnamed x0 -> x31, other arithmetic: none -> 7.07 us
where the time goes in v1:
time: 624 us; the launch traced here: 614 us
  waiting for transfers between devices  220 us (35%)
  local copies, waits for them, and re-layouts  153 us (25%)
  matrix products  85.1 us (14%)
  blocking collectives  81.8 us (13%)
  other arithmetic  34.5 us (6%)
  starting transfers between devices  24.8 us (4%)
  between operations  14.6 us (2%)
    unnamed x2, waiting for transfers between devices  146 us
    all_to_all x1, blocking collectives, on_device(): lax.all_to_all(jnp.stack(jnp.split(volume, lax.axis_size('slab'), axis=3)...  81.8 us
    reshape x3, local copies, waits for them, and re-layouts, on_device(): jnp.concatenate(lax.all_to_all(jnp.stack(jnp.split(volume, lax.axis_size(...  65.2 us
    unnamed x15, local copies, waits for them, and re-layouts  61.4 us
    all_to_all x1, waiting for transfers between devices, on_device(): lax.all_to_all(send_spec, 'slab', split_axis=0, concat_axis=0, tiled=True)  47.1 us
    all_to_all x1, waiting for transfers between devices, on_device(): lax.all_to_all(send_ctf, 'slab', split_axis=0, concat_axis=0, tiled=True)  21.3 us
    all_to_all x1, other arithmetic, on_device(): lax.all_to_all(jnp.stack(jnp.split(volume, lax.axis_size('slab'), axis=3)...  19.8 us
    dot_general x1, matrix products, inverse_kz(): jnp.einsum('zk,ykx->yzx', sine, imag_part, precision=highest)  19.3 us
  transfers between devices with their start and end apart: 5, of which 5 were waited for; matrix products, arithmetic and copies ran while one was open for 3% of the time, Pallas kernels for 0%

profile of v1, /device:TPU:1, one launch (start us, length us, event | category | flops | bytes accessed | tf_op | source)
XLA Modules:
  0.0 614.2 jit_solution(8456903932820175969)
XLA Ops:
  6.5 0.7 fusion.144
  7.2 1.2 reduce-window.6
  8.7 0.8 fusion.143
  9.4 0.7 compare_select_fusion
  10.1 0.7 convert_convert_fusion
  10.8 3.8 scatter_custom_fusion
  14.6 0.7 all_to_all.42
  15.3 8.6 %all-to-all-start = ((bf16[32,32,1]{1,2,0:T(2,128)(2,1)}), bf16[32,32,1]{1,2,0:T(2,128)(2,1)S(1)}, u32[]{:S(2)}, u32[]{:S(2)}) async-start(bf16[32,32,1]{1,2,0:T(2,128)(2,1)} %all_to_all.42), calls=%async_computation | async-start | bytes 32768 | tf_op jit(solution)/shard_map/all_to_all | solution.py:59
  23.9 0.9 convolution_convert_fusion
  25.0 1.8 scatter_custom_fusion.1
  27.0 0.7 reshape.157
  27.7 3.1 all-to-all-done
  30.8 4.2 all-to-all-start.1
  35.1 4.8 scatter_custom_fusion.3
  39.9 2.1 all-to-all-done.1
  42.0 5.9 all-to-all-start.3
  47.9 7.2 %scatter_custom_fusion.2 = bf16[1024,2048]{1,0:T(8,128)(2,1)} fusion(s32[512]{0:T(512)S(1)} %bitcast.256, bf16[512,2048]{1,0:T(8,128)(2,1)} %param.7, bf16[]{:T(256)} %constant.12.clone.1), kind=kCustom, calls=%fused_computation.85 | custom fusion | bytes 4194816 | tf_op jit(solution)/shard_map/scatter | solution.py:51
  55.1 21.3 %all-to-all-done.3 = bf16[32,32,1024]{2,1,0:T(8,128)(2,1)S(1)} async-done(((bf16[32,32,1024]{2,1,0:T(8,128)(2,1)}), bf16[32,32,1024]{2,1,0:T(8,128)(2,1)S(1)}, u32[]{:S(2)}, u32[]{:S(2)}) %all-to-all-start.3) | async-done | bytes 2097184 | tf_op jit(solution)/shard_map/all_to_all | solution.py:57
  76.4 6.1 all-to-all-start.2
  83.2 2.9 convolution_bitcast_fusion
  86.0 47.1 %all-to-all-done.2 = bf16[32,32,2048]{2,1,0:T(8,128)(2,1)} async-done(((bf16[32,32,2048]{2,1,0:T(8,128)(2,1)}), bf16[32,32,2048]{2,1,0:T(8,128)(2,1)}, u32[]{:S(2)}, u32[]{:S(2)}) %all-to-all-start.2) | async-done | bytes 4194336 | tf_op jit(solution)/shard_map/all_to_all | solution.py:56
  133.2 6.4 %copy.26 = bf16[2048,1024]{1,0:T(8,128)(2,1)} copy(bf16[2048,1024]{0,1:T(8,128)(2,1)} %bitcast.13) | data formatting | bytes 8388608 | tf_op jit(solution)/shard_map/dot_general | solution.py:69
  139.6 4.6 fusion.163
  144.3 0.3 fusion.50
  144.5 0.3 fusion.53
  144.8 0.3 fusion.56
  145.2 0.3 fusion.62
  145.4 0.3 fusion.65
  145.7 0.3 fusion.68
  146.1 0.3 fusion.74
  146.4 0.3 fusion.77
  146.7 0.3 fusion.80
  147.0 0.3 fusion.86
  147.3 0.3 fusion.89
  147.6 0.3 fusion.92
  148.0 0.3 fusion.98
  148.2 0.3 fusion.101
  148.5 0.3 fusion.104
  149.2 0.3 fusion.113
  149.4 0.3 fusion.116
  150.1 0.3 fusion.125
  150.4 0.3 fusion.128
  150.7 0.3 fusion.134
  151.0 0.3 fusion.44
  151.3 0.3 fusion.136
  151.6 8.3 %copy-done.2 = f32[32,16,32,3,32]{4,2,3,1,0:T(8,128)} copy-done((f32[32,16,32,3,32]{4,2,3,1,0:T(8,128)}, f32[32,16,32,3,32]{4,2,3,1,0:T(8,128)S(1)}, u32[]{:S(2)}) %copy-start.2) | copy-done | bytes 6291480
  159.9 27.1 %reshape.159 = f32[32,1,49152]{2,1,0:T(1,128)} reshape(f32[32,16,3,32,32]{4,3,2,1,0:T(8,128)} %bitcast.241) | data formatting | bytes 12582912
  187.0 81.8 %all_to_all.48 = f32[32,1,49152]{2,1,0:T(1,128)} all-to-all(f32[32,1,49152]{2,1,0:T(1,128)} %reshape.159), channel_id=1, replica_groups=mesh['grp'=8,'slab'=32] {'slab'}, dimensions={0} | all-to-all | bytes 12582912 | tf_op jit(solution)/shard_map/all_to_all | solution.py:75
  268.8 0.5 broadcast.112
  269.3 19.8 %reduce.6 = f32[32,49152]{1,0:T(8,128)} reduce(f32[32,1,49152]{2,1,0:T(1,128)} %all_to_all.48, f32[]{:T(128)} %broadcast.112), dimensions={1}, to_apply=%all_to_all.41.reduce_sub_computation | reduce | bytes 12582916 | tf_op jit(solution)/shard_map/all_to_all | solution.py:75
  289.1 24.5 %reshape.160 = f32[32,16,3,32,32]{4,3,2,1,0:T(8,128)} reshape(f32[32,49152]{1,0:T(8,128)} %reduce.6) | data formatting | bytes 12582912
  313.6 18.0 %bitcast_bitcast_fusion.1 = f32[16,32,32,3,32]{4,2,3,0,1:T(8,128)} fusion(f32[32,16,3,32,32]{4,3,2,1,0:T(8,128)} %reshape.160), kind=kLoop, calls=%fused_computation.236 | loop fusion | bytes 12582912 | tf_op jit(solution)/shard_map/reshape | solution.py:74
  331.7 27.1 %copy.30 = f32[16,32,32,3,32]{2,1,4,0,3:T(8,128)} copy(f32[16,32,32,3,32]{4,2,3,0,1:T(8,128)} %bitcast_bitcast_fusion.1) | data formatting | bytes 12582912 | tf_op jit(solution)/shard_map/reshape | solution.py:74
  358.7 20.1 %reshape.137 = f32[16,1024,3,32]{1,3,0,2:T(8,128)} reshape(f32[16,32,32,3,32]{2,1,4,0,3:T(8,128)} %copy.30) | data formatting | bytes 12582912 | tf_op jit(solution)/shard_map/reshape | solution.py:74
  378.9 0.8 dynamic_slice.3
  379.7 0.6 dynamic-slice
  380.9 146.4 %all-reduce.3.cloned.1.call-done = f32[16,1024,3,32]{1,3,0,2:T(8,128)} async-done(((f32[16,1024,3,32]{1,3,0,2:T(8,128)}), f32[16,1024,3,32]{1,3,0,2:T(8,128)}) %all-reduce.3.cloned.1.call-update) | async-done | bytes 6291472
  527.3 1.0 fusion.137
  528.3 1.1 dynamic-slice_divide_fusion
  529.4 19.3 %fusion.5 = f32[2,32,1024]{2,1,0:T(8,128)S(1)} fusion(f32[2,1024,2,32]{1,3,0,2:T(8,128)S(1)} %dynamic-slice_divide_fusion), kind=kOutput, calls=%fused_computation.74 | convolution fusion | flops 819986432 | bytes 524288 | tf_op jit(solution)/shard_map/zk,ykx->yzx/dot_general | solution.py:24
  548.7 19.2 %fusion.3 = f32[2,32,1024]{2,1,0:T(8,128)S(1)} fusion(f32[2,1024,2,32]{1,3,0,2:T(8,128)S(1)} %dynamic-slice_divide_fusion), kind=kOutput, calls=%fused_computation.72 | convolution fusion | flops 819986432 | bytes 524288 | tf_op jit(solution)/shard_map/zk,ykx->yzx/dot_general | solution.py:27
  568.0 19.1 %fusion.37 = f32[1,2,1024,32]{2,3,1,0:T(8,128)S(1)} fusion(f32[2,32,1024]{2,1,0:T(8,128)S(1)} %fusion.5, f32[2,1024,2,32]{1,3,0,2:T(8,128)S(1)} %dynamic-slice_divide_fusion), kind=kOutput, calls=%fused_computation.93 | convolution fusion | flops 820117504 | bytes 786432 | tf_op jit(solution)/shard_map/zk,ykx->yzx/dot_general | solution.py:24
  587.2 19.1 %fusion.31 = f32[1,2,1024,32]{2,3,1,0:T(8,128)S(1)} fusion(f32[2,32,1024]{2,1,0:T(8,128)S(1)} %fusion.3, f32[2,1024,2,32]{1,3,0,2:T(8,128)S(1)} %dynamic-slice_divide_fusion), kind=kOutput, calls=%fused_computation.91 | convolution fusion | flops 820117504 | bytes 786432 | tf_op jit(solution)/shard_map/zk,ykx->yzx/dot_general | solution.py:27
  606.3 0.8 pad_maximum_fusion.1
  (34 shorter events, 2.6 us)
Async XLA Ops:
  6.5 17.3 %copy-start = (bf16[64,8]{0,1:T(8,128)(2,1)S(1)}, bf16[64,8]{0,1:T(8,128)(2,1)}, u32[]{:S(2)}) copy-start(bf16[64,8]{0,1:T(8,128)(2,1)} %param.12) | copy-start | bytes 3076
  15.3 15.6 %all-to-all-start = ((bf16[32,32,1]{1,2,0:T(2,128)(2,1)}), bf16[32,32,1]{1,2,0:T(2,128)(2,1)S(1)}, u32[]{:S(2)}, u32[]{:S(2)}) async-start(bf16[32,32,1]{1,2,0:T(2,128)(2,1)} %all_to_all.42), calls=%async_computation | async-start | bytes 32768 | tf_op jit(solution)/shard_map/all_to_all | solution.py:59
  30.8 11.1 %all-to-all-start.1 = ((bf16[32,2,128]{2,1,0:T(2,128)(2,1)}), bf16[32,2,128]{2,1,0:T(2,128)(2,1)S(1)}, u32[]{:S(2)}, u32[]{:S(2)}) async-start(bf16[32,2,128]{2,1,0:T(2,128)(2,1)} %reshape.157), calls=%async_computation.1 | async-start | bytes 32768 | tf_op jit(solution)/shard_map/all_to_all | solution.py:58
  42.0 34.4 %all-to-all-start.3 = ((bf16[32,32,1024]{2,1,0:T(8,128)(2,1)}), bf16[32,32,1024]{2,1,0:T(8,128)(2,1)S(1)}, u32[]{:S(2)}, u32[]{:S(2)}) async-start(bf16[32,32,1024]{2,1,0:T(8,128)(2,1)} %bitcast.18), calls=%async_computation.3 | async-start | bytes 4194304 | tf_op jit(solution)/shard_map/all_to_all | solution.py:57
  76.4 6.8 %copy-start.3 = (bf16[32,32,1024]{2,1,0:T(8,128)(2,1)}, bf16[32,32,1024]{2,1,0:T(8,128)(2,1)S(1)}, u32[]{:S(2)}) copy-start(bf16[32,32,1024]{2,1,0:T(8,128)(2,1)S(1)} %all-to-all-done.3) | copy-start | bytes 6291460
  76.4 56.8 %all-to-all-start.2 = ((bf16[32,32,2048]{2,1,0:T(8,128)(2,1)}), bf16[32,32,2048]{2,1,0:T(8,128)(2,1)}, u32[]{:S(2)}, u32[]{:S(2)}) async-start(bf16[32,32,2048]{2,1,0:T(8,128)(2,1)} %bitcast.242), calls=%async_computation.2 | async-start | bytes 8388608 | tf_op jit(solution)/shard_map/all_to_all | solution.py:56
  82.5 444.8 %all-reduce.3.cloned.1.call-start = ((), (), s32[]{:S(2)}) async-start(), calls=%async_computation.5 | async-start | bytes 12582912
  151.6 8.3 %copy-start.2 = (f32[32,16,32,3,32]{4,2,3,1,0:T(8,128)}, f32[32,16,32,3,32]{4,2,3,1,0:T(8,128)S(1)}, u32[]{:S(2)}) copy-start(f32[32,16,32,3,32]{4,2,3,1,0:T(8,128)S(1)} %fusion.136) | copy-start | bytes 18874372
  378.8 0.8 copy-start.4
  568.0 39.1 %copy-start.1 = (bf16[64,8]{0,1:T(8,128)(2,1)S(1)}, bf16[64,8]{0,1:T(8,128)(2,1)}, u32[]{:S(2)}) copy-start(bf16[64,8]{0,1:T(8,128)(2,1)} %param.12) | copy-start | bytes 3076
Sparse Core Ops, SparseCore 0:
  379.0 148.2 all-reduce.2
